TPU v7x, 512 devices: a whole 4x4x16 slice. The times are simulated.
512 devices in a mesh: ka: 16 (over y, z_hi), row: 4 (over x), col: 8 (over z_lo, core).
Axes of the slice: x: 4, y: 4, z: 16 (z_hi: 4, z_lo: 4; z = z_hi * 4 + z_lo), core: 2. Of those that a mesh axis runs over, the one named last changes fastest.
Arguments:
- exciton: bfloat16 [16, 4, 128, 128], P('ka'), may hold values from -6 to 6
- orb_cond: bfloat16 [16, 128, 2048], P('ka', None, 'row'), may hold values from -0.5 to 0.5
- orb_val: bfloat16 [16, 128, 2048], P('ka', None, 'col'), may hold values from -0.5 to 0.5
- screened: bfloat16 [16, 2048, 2048], P(None, 'row', 'col'), may hold values from -1.5 to 1.5
- q_table: int32 [16, 16], replicated, may hold values from 0 to 15, as said below
Outputs:
- applied: float32 [16, 4, 128, 128], P('ka', None, 'col')
Inputs may be any that keep to these rules, and one draw needn't show every extreme that they name: q_table is the difference table of the k-points of a cyclic grid of 16 points under a relabeling of points and of differences: every row and every column holds each of 0 to 15 once.
All inputs are finite; a program needn't handle non-finite values.
Results may differ from a plain program's by a relative error of at most 0.019.
Values may be sent and summed in bfloat16 or wider, within the bound.
A program may use at most 64 MiB of HBM per device.

v0:
```python
import math
import jax
import jax.numpy as jnp
from jax import lax
from jax.sharding import PartitionSpec as P

NV = 128
NC = 128
NMU = 2048


def split_up(x, dim, devices):
    before, after = (x.shape[:dim], x.shape[dim + 1 :])
    return jnp.moveaxis(x.reshape(*before, devices, -1, *after), dim, 0)


def summed_on_arrival(x, axis, dim):
    blocks = split_up(x, dim, lax.axis_size(axis))
    arrived = lax.all_to_all(blocks, axis, split_axis=0, concat_axis=0, tiled=True)
    return arrived.astype(jnp.float32).sum(axis=0)


def copy_for_each(x, axis):
    devices = lax.axis_size(axis)
    return lax.all_to_all(jnp.broadcast_to(x[None], (devices, *x.shape)), axis, 0, 0, tiled=True)


def of_everyone(x, axis):
    return copy_for_each(x, axis).astype(jnp.float32).sum(axis=0)


def local(exciton, orb_cond, orb_val, screened, q_table):
    local_count = exciton.shape[0]
    own_points = lax.axis_index("ka") * local_count + jnp.arange(local_count, dtype=jnp.int32)
    q_columns = jnp.take(q_table, own_points, axis=1)
    panels = jnp.einsum(
        "kbvc,kcm->kbvm", exciton, orb_cond, preferred_element_type=jnp.float32
    ).astype(jnp.bfloat16)
    start_sum = jnp.zeros(
        (local_count, exciton.shape[1], orb_cond.shape[2], orb_val.shape[2]), jnp.float32
    )

    def weigh_pairs(running, pair_block, position):
        indices = lax.dynamic_index_in_dim(q_columns, position, 0, keepdims=False)
        weights = jnp.take(screened, indices, axis=0).astype(jnp.float32)
        return running + weights[:, None] * pair_block[None].astype(jnp.float32)

    portion = (
        lax.all_gather(panels, "ka", axis=0, tiled=True),
        lax.all_gather(orb_val, "ka", axis=0, tiled=True),
    )

    def one_point(entry_index, inner_sum):
        panel_rows = lax.dynamic_index_in_dim(portion[0], entry_index, 0, keepdims=False)
        valence = lax.dynamic_index_in_dim(portion[1], entry_index, 0, keepdims=False)
        pair_block = jnp.einsum(
            "bvm,vn->bmn", panel_rows, valence, preferred_element_type=jnp.float32
        ).astype(jnp.bfloat16)
        return weigh_pairs(inner_sum, pair_block, entry_index)

    direct = lax.fori_loop(0, portion[0].shape[0], one_point, start_sum)
    direct = direct.astype(jnp.bfloat16)
    half_sums = jnp.einsum(
        "kbmn,kvn->kbmv", direct, orb_val, preferred_element_type=jnp.float32
    ).astype(jnp.bfloat16)
    factor = math.sqrt(NV * NC) / NMU
    partial_value = (
        jnp.einsum("kcm,kbmv->kbvc", orb_cond, half_sums, preferred_element_type=jnp.float32)
        * factor
    )
    shares = summed_on_arrival(partial_value.astype(jnp.bfloat16), "col", 2)
    result = of_everyone(shares.astype(jnp.bfloat16), "row").astype(jnp.float32)
    return result


def solution(mesh):
    placed = (
        P("ka", None, None, None),
        P("ka", None, "row"),
        P("ka", None, "col"),
        P(None, "row", "col"),
        P(),
    )
    return jax.shard_map(
        local, mesh=mesh, in_specs=placed, out_specs=P("ka", None, "col", None), check_vma=False
    )
```

profile of v0, /device:TPU:8, one launch (start us, length us, event | category | flops | bytes accessed | tf_op | source)
XLA Modules:
  0.0 422.1 jit_solution(8037367269032499573)
XLA Ops:
  6.5 0.7 all-gather.4.cloned.1.call-update
  7.4 2.0 convolution_convert_fusion.2
  9.4 0.8 constant_dynamic-slice_fusion.1
  10.3 81.8 %all-gather.4.cloned.1.call-done = bf16[16,128,256]{2,1,0:T(8,128)(2,1)} async-done(((bf16[1,128,256]{2,1,0:T(8,128)(2,1)}), bf16[16,128,256]{2,1,0:T(8,128)(2,1)}) %all-gather.4.cloned.1.call-update) | async-done | bytes 1048592 | tf_op jit(solution)/shard_map/all_gather | solution.py:50
  92.1 215.3 %all-gather.6.cloned.1.call-done = bf16[64,128,512]{2,1,0:T(8,128)(2,1)} async-done(((bf16[4,128,512]{2,1,0:T(8,128)(2,1)}), bf16[64,128,512]{2,1,0:T(8,128)(2,1)}) %all-gather.6.cloned.1.call-update) | async-done | bytes 8388624 | tf_op jit(solution)/shard_map/all_gather | solution.py:49
  307.4 86.6 %while.16 = (s32[]{:T(128)}, f32[1,4,512,256]{3,2,1,0:T(8,128)S(1)}, s32[16,1]{0,1:T(1,128)S(1)}, bf16[16,512,256]{2,1,0:T(8,128)(2,1)}, bf16[16,4,128,512]{3,2,...) while((s32[]{:T(128)}, ...), condition=%wide.region_1.2_spmd.clone, body=%wide.region_0.1_spmd.clone.sunk | while | flops 137101312 | bytes 6096063 | solution.py:61
  309.9 1.0 bitcast_convert_fusion.2
  310.9 1.9 bitcast_add_fusion.2
  312.8 0.6 constant_dynamic-slice_fusion.3
  315.3 1.0 bitcast_convert_fusion.2
  316.3 1.9 bitcast_add_fusion.2
  318.3 0.6 constant_dynamic-slice_fusion.3
  320.7 1.0 bitcast_convert_fusion.2
  321.7 1.9 bitcast_add_fusion.2
  323.7 0.6 constant_dynamic-slice_fusion.3
  326.2 1.0 bitcast_convert_fusion.2
  327.2 1.9 bitcast_add_fusion.2
  329.1 0.6 constant_dynamic-slice_fusion.3
  331.6 1.0 bitcast_convert_fusion.2
  332.6 1.9 bitcast_add_fusion.2
  334.5 0.6 constant_dynamic-slice_fusion.3
  337.0 1.0 bitcast_convert_fusion.2
  338.0 1.9 bitcast_add_fusion.2
  342.4 1.0 bitcast_convert_fusion.2
  343.4 1.9 bitcast_add_fusion.2
  347.8 1.0 bitcast_convert_fusion.2
  348.8 1.9 bitcast_add_fusion.2
  353.2 1.0 bitcast_convert_fusion.2
  354.2 1.9 bitcast_add_fusion.2
  358.7 1.0 bitcast_convert_fusion.2
  359.7 1.9 bitcast_add_fusion.2
  361.6 0.6 constant_dynamic-slice_fusion.3
  364.1 1.0 bitcast_convert_fusion.2
  365.1 1.9 bitcast_add_fusion.2
  369.5 1.0 bitcast_convert_fusion.2
  370.5 1.9 bitcast_add_fusion.2
  374.9 1.0 bitcast_convert_fusion.2
  375.9 1.9 bitcast_add_fusion.2
  380.3 1.0 bitcast_convert_fusion.2
  381.3 1.9 bitcast_add_fusion.2
  385.7 1.0 bitcast_convert_fusion.2
  386.7 1.9 bitcast_add_fusion.2
  391.1 1.0 bitcast_convert_fusion.2
  392.1 1.9 bitcast_add_fusion.2
  394.1 0.8 fusion.7
  395.0 10.0 %all_to_all.10 = bf16[8,1,4,16,128]{4,3,2,1,0:T(8,128)(2,1)S(1)} all-to-all(bf16[8,1,4,16,128]{4,3,2,1,0:T(8,128)(2,1)S(1)} %bitcast.59), channel_id=1, replica_groups=mesh['ka'=16,'row'=4,'col'=8] {'col'}, dimensions={0} | all-to-all | bytes 262144 | tf_op jit(solution)/shard_map/all_to_all | solution.py:19
  405.0 9.7 %all_to_all.11 = bf16[4,1,4,16,128]{4,3,2,1,0:T(8,128)(2,1)S(1)} all-to-all(bf16[4,1,4,16,128]{4,3,2,1,0:T(8,128)(2,1)S(1)} %broadcast_in_dim.46), channel_id=1, replica_groups=mesh['ka'=16,'row'=4,'col'=8] {'row'}, dimensions={0} | all-to-all | bytes 131072 | tf_op jit(solution)/shard_map/all_to_all | solution.py:25
  414.7 0.6 convert_reduce_fusion
  (23 shorter events, 6.3 us)
Async XLA Ops:
  6.5 0.9 copy-start
  6.5 85.6 %all-gather.4.cloned.1.call-start = ((), (), s32[]{:S(2)}) async-start(), calls=%async_computation.2 | async-start | bytes 1114112 | tf_op jit(solution)/shard_map/all_gather | solution.py:50
  7.3 300.2 %all-gather.6.cloned.1.call-start = ((), (), s32[]{:S(2)}) async-start(), calls=%async_computation.3 | async-start | bytes 8912896 | tf_op jit(solution)/shard_map/all_gather | solution.py:49
  307.4 86.6 %copy-start.1 = (bf16[1,128,256]{2,1,0:T(8,128)(2,1)S(1)}, bf16[1,128,256]{2,1,0:T(8,128)(2,1)}, u32[]{:S(2)}) copy-start(bf16[1,128,256]{2,1,0:T(8,128)(2,1)} %param.9) | copy-start | bytes 196612
Sparse Core Ops, SparseCore 0:
  10.3 81.7 all-gather.3
  95.1 212.2 all-gather.5
where the time goes:
time: 424 us; the launch traced here: 422 us
  waiting for transfers between devices  298 us (70%)
  matrix products  33.4 us (8%)
  loops' own time  30.6 us (7%)
  blocking collectives  19.7 us (5%)
  other arithmetic  16.5 us (4%)
  between operations  13.5 us (3%)
  local copies, waits for them, and re-layouts  10.5 us (2%)
    all_gather x1, waiting for transfers between devices, local(): lax.all_gather(panels, 'ka', axis=0, tiled=True)  215 us
    all_gather x1, waiting for transfers between devices, local(): lax.all_gather(orb_val, 'ka', axis=0, tiled=True)  81.8 us
    dot_general x16, matrix products, one_point(): jnp.einsum('bvm,vn->bmn', panel_rows, valence, preferred_element_type=jnp...  30.6 us
    another operation x1, loops' own time, local(): direct = lax.fori_loop(0, portion[0].shape[0], one_point, start_sum)  30.6 us
    convert_element_type x16, other arithmetic, weigh_pairs(): weights = jnp.take(screened, indices, axis=0).astype(jnp.float32)  15.9 us
    all_to_all x1, blocking collectives, summed_on_arrival(): lax.all_to_all(blocks, axis, split_axis=0, concat_axis=0, tiled=True)  9.99 us
    all_to_all x1, blocking collectives, copy_for_each(): lax.all_to_all(jnp.broadcast_to(x[None], (devices, *x.shape)), axis, 0, 0...  9.67 us
    dynamic_slice x16, local copies, waits for them, and re-layouts, weigh_pairs(): indices = lax.dynamic_index_in_dim(q_columns, position, 0, keepdims=False)  9.52 us
  transfers between devices with their start and end apart: 2, of which 2 were waited for; matrix products, arithmetic and copies ran while one was open for 1% of the time, Pallas kernels for 0%

commit v1 on v0

--- a/solution.py
+++ b/solution.py
@@ -7,6 +7,11 @@
 NV = 128
 NC = 128
 NMU = 2048
+
+
+def gather_over(x, mesh_axis, d):
+    repeated = jnp.stack([x] * lax.axis_size(mesh_axis))
+    return jnp.concatenate(lax.all_to_all(repeated, mesh_axis, 0, 0), axis=d)
 
 
 def split_up(x, dim, devices):
@@ -45,10 +50,7 @@
         weights = jnp.take(screened, indices, axis=0).astype(jnp.float32)
         return running + weights[:, None] * pair_block[None].astype(jnp.float32)
 
-    portion = (
-        lax.all_gather(panels, "ka", axis=0, tiled=True),
-        lax.all_gather(orb_val, "ka", axis=0, tiled=True),
-    )
+    portion = (gather_over(panels, "ka", 0), lax.all_gather(orb_val, "ka", axis=0, tiled=True))
 
     def one_point(entry_index, inner_sum):
         panel_rows = lax.dynamic_index_in_dim(portion[0], entry_index, 0, keepdims=False)

time: 424 us -> 551 us (1.30)
  waiting for transfers between devices: 298 us -> 386 us
  starting transfers between devices: 0.04 us -> 18.3 us
  blocking collectives: 19.7 us -> 34.2 us
  local copies, waits for them, and re-layouts: 10.5 us -> 17.1 us
    all_gather x1 -> x0, waiting for transfers between devices: 215 us -> none  [local(): lax.all_gather(panels, 'ka', axis=0, tiled=True)]
    all_to_all x0 -> x1, waiting for transfers between devices: none -> 205 us  [gather_over(): return jnp.concatenate(lax.all_to_all(repeated, mesh_axis, 0, 0), axis=d)]
    all_gather x1, waiting for transfers between devices: 81.8 us -> 181 us  [local(): lax.all_gather(orb_val, 'ka', axis=0, tiled=True)]
    all_to_all x0 -> x1, starting transfers between devices: none -> 18.3 us  [gather_over(): return jnp.concatenate(lax.all_to_all(repeated, mesh_axis, 0, 0), axis=d)]
    all_to_all x1, blocking collectives: 9.99 us -> 18.8 us  [summed_on_arrival(): lax.all_to_all(blocks, axis, split_axis=0, concat_axis=0, tiled=True)]
    all_to_all x1, blocking collectives: 9.67 us -> 15.4 us  [copy_for_each(): lax.all_to_all(jnp.broadcast_to(x[None], (devices, *x.shape)), axis, 0, 0...]
  transfers between devices with their start and end apart: 2 -> 2, of which waited for: 2 -> 2; matrix products, arithmetic and copies ran while one was open for 1% -> 0% of each run, Pallas kernels for 0% -> 0%
where the time goes in v1:
time: 551 us; the launch traced here: 550 us
  waiting for transfers between devices  386 us (70%)
  blocking collectives  34.2 us (6%)
  loops' own time  33.1 us (6%)
  matrix products  30.9 us (6%)
  starting transfers between devices  18.3 us (3%)
  local copies, waits for them, and re-layouts  17.1 us (3%)
  other arithmetic  16.5 us (3%)
  between operations  13.5 us (2%)
    all_to_all x1, waiting for transfers between devices, gather_over(): return jnp.concatenate(lax.all_to_all(repeated, mesh_axis, 0, 0), axis=d)  205 us
    all_gather x1, waiting for transfers between devices, local(): lax.all_gather(orb_val, 'ka', axis=0, tiled=True)  181 us
    another operation x1, loops' own time, local(): direct = lax.fori_loop(0, portion[0].shape[0], one_point, start_sum)  33.1 us
    dot_general x16, matrix products, one_point(): jnp.einsum('bvm,vn->bmn', panel_rows, valence, preferred_element_type=jnp...  28.9 us
    all_to_all x1, blocking collectives, summed_on_arrival(): lax.all_to_all(blocks, axis, split_axis=0, concat_axis=0, tiled=True)  18.8 us
    all_to_all x1, starting transfers between devices, gather_over(): return jnp.concatenate(lax.all_to_all(repeated, mesh_axis, 0, 0), axis=d)  18.3 us
    convert_element_type x16, other arithmetic, weigh_pairs(): weights = jnp.take(screened, indices, axis=0).astype(jnp.float32)  15.9 us
    all_to_all x1, blocking collectives, copy_for_each(): lax.all_to_all(jnp.broadcast_to(x[None], (devices, *x.shape)), axis, 0, 0...  15.4 us
  transfers between devices with their start and end apart: 2, of which 2 were waited for; matrix products, arithmetic and copies ran while one was open for 0% of the time, Pallas kernels for 0%

profile of v1, /device:TPU:8, one launch (start us, length us, event | category | flops | bytes accessed | tf_op | source)
XLA Modules:
  0.0 549.6 jit_solution(11455147473228186166)
XLA Ops:
  6.5 0.9 copy-done
  7.4 1.2 convolution_convert_fusion.2
  8.9 5.3 stack.2
  14.2 18.3 %all-to-all-start = ((bf16[16,1,4,128,512]{3,4,2,1,0:T(8,128)(2,1)}), bf16[16,1,4,128,512]{3,4,2,1,0:T(8,128)(2,1)}, u32[]{:S(2)}, u32[]{:S(2)}) async-start(bf16[16,1,4,128,512]{3,4,2,1,0:T(8,128)(2,1)} %stack.2), calls=%async_computation | async-start | bytes 16777216 | tf_op jit(solution)/shard_map/all_to_all | solution.py:14
  32.6 0.7 all-gather.2.cloned.1.call-update
  33.5 180.5 %all-gather.2.cloned.1.call-done = bf16[16,128,256]{2,1,0:T(8,128)(2,1)} async-done(((bf16[1,128,256]{2,1,0:T(8,128)(2,1)}), bf16[16,128,256]{2,1,0:T(8,128)(2,1)}) %all-gather.2.cloned.1.call-update) | async-done | bytes 1048592 | tf_op jit(solution)/shard_map/all_gather | solution.py:53
  214.0 204.6 %all-to-all-done = bf16[16,1,4,128,512]{3,4,2,1,0:T(8,128)(2,1)} async-done(((bf16[16,1,4,128,512]{3,4,2,1,0:T(8,128)(2,1)}), bf16[16,1,4,128,512]{3,4,2,1,0:T(8,128)(2,1)}, u32[]{:S(2)}, u32[]{:S(2)}) %all-to-all-start) | async-done | bytes 8388640 | tf_op jit(solution)/shard_map/all_to_all | solution.py:14
  418.6 88.3 %while.16 = (s32[]{:T(128)}, f32[1,4,512,256]{3,2,1,0:T(8,128)S(1)}, s32[16,1]{0,1:T(1,128)S(1)}, bf16[16,512,256]{2,1,0:T(8,128)(2,1)}, bf16[16,4,128,512]{2,3,...) while((s32[]{:T(128)}, ...), condition=%wide.region_1.2_spmd.clone, body=%wide.region_0.1_spmd.clone.sunk | while | flops 137101312 | bytes 6096063 | solution.py:63
  421.3 1.0 bitcast_convert_fusion.2
  422.3 1.8 bitcast_add_fusion.2
  424.2 0.7 constant_dynamic-slice_fusion.3
  426.9 1.0 bitcast_convert_fusion.2
  427.9 1.8 bitcast_add_fusion.2
  429.7 0.7 constant_dynamic-slice_fusion.3
  432.4 1.0 bitcast_convert_fusion.2
  433.4 1.8 bitcast_add_fusion.2
  435.2 0.7 constant_dynamic-slice_fusion.3
  437.9 1.0 bitcast_convert_fusion.2
  438.9 1.8 bitcast_add_fusion.2
  440.7 0.7 constant_dynamic-slice_fusion.3
  443.4 1.0 bitcast_convert_fusion.2
  444.4 1.8 bitcast_add_fusion.2
  446.2 0.7 constant_dynamic-slice_fusion.3
  448.9 1.0 bitcast_convert_fusion.2
  449.9 1.8 bitcast_add_fusion.2
  454.5 1.0 bitcast_convert_fusion.2
  455.5 1.8 bitcast_add_fusion.2
  460.0 1.0 bitcast_convert_fusion.2
  461.0 1.8 bitcast_add_fusion.2
  465.5 1.0 bitcast_convert_fusion.2
  466.5 1.8 bitcast_add_fusion.2
  471.0 1.0 bitcast_convert_fusion.2
  472.0 1.8 bitcast_add_fusion.2
  476.5 1.0 bitcast_convert_fusion.2
  477.5 1.8 bitcast_add_fusion.2
  482.1 1.0 bitcast_convert_fusion.2
  483.1 1.8 bitcast_add_fusion.2
  487.6 1.0 bitcast_convert_fusion.2
  488.6 1.8 bitcast_add_fusion.2
  493.1 1.0 bitcast_convert_fusion.2
  494.1 1.8 bitcast_add_fusion.2
  498.6 1.0 bitcast_convert_fusion.2
  499.6 1.8 bitcast_add_fusion.2
  504.1 1.0 bitcast_convert_fusion.2
  505.1 1.8 bitcast_add_fusion.2
  507.0 0.8 fusion.7
  507.8 18.8 %all_to_all.15 = bf16[8,1,4,16,128]{4,3,2,1,0:T(8,128)(2,1)S(1)} all-to-all(bf16[8,1,4,16,128]{4,3,2,1,0:T(8,128)(2,1)S(1)} %bitcast.57), channel_id=1, replica_groups=mesh['ka'=16,'row'=4,'col'=8] {'col'}, dimensions={0} | all-to-all | bytes 262144 | tf_op jit(solution)/shard_map/all_to_all | solution.py:24
  526.7 15.4 %all_to_all.16 = bf16[4,1,4,16,128]{4,3,2,1,0:T(8,128)(2,1)S(1)} all-to-all(bf16[4,1,4,16,128]{4,3,2,1,0:T(8,128)(2,1)S(1)} %broadcast_in_dim.46), channel_id=1, replica_groups=mesh['ka'=16,'row'=4,'col'=8] {'row'}, dimensions={0} | all-to-all | bytes 131072 | tf_op jit(solution)/shard_map/all_to_all | solution.py:30
  (26 shorter events, 8.3 us)
Async XLA Ops:
  6.5 0.9 copy-start
  14.2 19.1 %copy-start.2 = (s32[16,16]{1,0:T(8,128)S(1)}, s32[16,16]{1,0:T(8,128)}, u32[]{:S(2)}) copy-start(s32[16,16]{1,0:T(8,128)} %param.11) | copy-start | bytes 3076
  14.2 404.4 %all-to-all-start = ((bf16[16,1,4,128,512]{3,4,2,1,0:T(8,128)(2,1)}), bf16[16,1,4,128,512]{3,4,2,1,0:T(8,128)(2,1)}, u32[]{:S(2)}, u32[]{:S(2)}) async-start(bf16[16,1,4,128,512]{3,4,2,1,0:T(8,128)(2,1)} %stack.2), calls=%async_computation | async-start | bytes 16777216 | tf_op jit(solution)/shard_map/all_to_all | solution.py:14
  32.5 181.5 %all-gather.2.cloned.1.call-start = ((), (), s32[]{:S(2)}) async-start(), calls=%async_computation.3 | async-start | bytes 1114112 | tf_op jit(solution)/shard_map/all_gather | solution.py:53
  418.6 88.3 %copy-start.1 = (bf16[1,128,256]{2,1,0:T(8,128)(2,1)S(1)}, bf16[1,128,256]{2,1,0:T(8,128)(2,1)}, u32[]{:S(2)}) copy-start(bf16[1,128,256]{2,1,0:T(8,128)(2,1)} %param.9) | copy-start | bytes 196612
Sparse Core Ops, SparseCore 0:
  36.4 177.5 all-gather.1
